TPU v7x, 32 devices: a whole 2x2x4 slice. The times are simulated.
32 devices in a mesh: group: 4 (over z), leaf: 8 (over y, x, core).
Axes of the slice: x: 2, y: 2, z: 4, core: 2. Of those that a mesh axis runs over, the one named last changes fastest.
Arguments:
- observations: float32 [64, 32768], P(None, ('group', 'leaf')), may hold values from -6 to 6
- coordinates: float32 [3, 32768], P(None, ('group', 'leaf')), may hold values from 0 to 8, as said below
- proxies: float32 [32, 3, 64], P(('group', 'leaf')), may hold values from 0 to 8, as said below
- noise_variance: float32 [32768], P(('group', 'leaf')), may hold values from 0.5 to 2
- ordering: int32 [32, 1024], P(('group', 'leaf')), may hold values from 0 to 1023, each once within a row
- near_list: int32 [32, 7], P(('group', 'leaf')), may hold values from 0 to 31, as said below
- far_within: int32 [32, 6], P(('group', 'leaf')), may hold values from 0 to 7, as said below
- far_across: int32 [32, 3, 2], P(('group', 'leaf')), may hold values from 0 to 7, as said below
- couplings: bfloat16 [32, 12, 64, 64], P(('group', 'leaf')), may hold values from -0.4375 to 0.4375
Outputs:
- gain: float32 [64, 32768], P(None, ('group', 'leaf'))
- residual: float32 [64, 32768], P(None, ('group', 'leaf'))
Inputs may be any that keep to these rules, and one draw needn't show every extreme that they name: `near_list`: row L names seven distinct leaves (L + d) mod 32 with d among -4, -3, -2, -1, 1, 2, 3, 4, in ascending order of d; the missing d is drawn for each leaf on its own and may be the same for different leaves. `far_within`: row L names 6 distinct leaves of L's own group by their index within the group, never L itself. `far_across`: entry [L, k, a] names, by its index within the group, a leaf of the group k + 1 places after L's own group, modulo the number of groups; the 2 entries of one [L, k] are distinct. Point coordinate 0 of leaf L lies in [L / 4, (L + 1) / 4]; coordinates 1 and 2 lie in [0, 8]. `proxies`: proxy coordinate 0 of leaf L lies in [L / 4, (L + 1) / 4]; coordinates 1 and 2 lie in [0, 8].
All inputs are finite; a program needn't handle non-finite values.
Results may differ from a plain program's by a relative error of at most 0.0045.
Values may be sent and summed in bfloat16 or wider, within the bound.
A program may use at most 128 MiB of HBM per device.

v0:
```python
import functools
import math

import jax
import jax.numpy as jnp
from jax import lax
from jax.experimental import pallas as pl
from jax.experimental.pallas import tpu as pltpu
from jax.sharding import PartitionSpec as P

length_scale = 0.5
kernel_scale = 8.0
lower_bound = 0.5
upper_bound = 4.0
REACH = 4
SPAN = 2 * REACH + 1
HOPS = (-4, -2, 2, 4)
SLAB = 0.25
SIDE = 8.0
SCALE = 1.0 / (length_scale * math.log(2.0))
TINY = 1e-12
BLOCK = 256
ROWS = 8
DEPTH = 128
MESH = pl.DeviceIdType.MESH
F32 = jnp.float32
BF16 = jnp.bfloat16

LAST = (((1,), (1,)), ((), ()))


def dot(a, b):
    return jnp.dot(a, b, preferred_element_type=F32)


def dot_last(a, b):
    return lax.dot_general(a, b, LAST, preferred_element_type=F32)


def split3(x):
    high = x.astype(BF16).astype(F32)
    rest = x - high
    mid = rest.astype(BF16).astype(F32)
    low = (rest - mid).astype(BF16).astype(F32)
    return high, mid, low


def eight(coords):
    return jnp.concatenate(
        [coords, jnp.zeros((ROWS - coords.shape[0], coords.shape[1]), F32)], axis=0
    )


def features(coords, shift0):
    row = lax.broadcasted_iota(jnp.int32, coords.shape, 0)
    shift = jnp.where(row == 0, shift0, SIDE / 2)
    x = jnp.where(row < 3, (coords - shift) * SCALE, 0.0)
    h, m, l = split3(x)
    n1, n2, n3 = split3(jnp.sum(x * x, axis=0, keepdims=True))
    one = jnp.ones_like(x)
    zero = jnp.zeros_like(x)
    left = jnp.where(row == 0, n1, jnp.where(row == 1, n2, n3))
    left = jnp.where(row < 3, left, jnp.where(row < 6, one, zero))
    right = jnp.where(row == 3, n1, jnp.where(row == 4, n2, n3))
    right = jnp.where(row < 3, one, jnp.where(row < 6, right, zero))
    pad = [zero] * (DEPTH // ROWS - 10)
    source = jnp.concatenate([h, h, h, m, m, m, l, l, l, left] + pad, axis=0)
    h2, m2, l2 = -2.0 * h, -2.0 * m, -2.0 * l
    target = jnp.concatenate([h2, m2, l2, h2, m2, l2, h2, m2, l2, right] + pad, axis=0)
    return source, target


def from_squares(s):
    s = jnp.maximum(s, TINY)
    return jnp.exp2(-(s * lax.rsqrt(s))).astype(BF16)


def kernel(
    n_group,
    n_leaf,
    obs_ref,
    coords_ref,
    prox_ref,
    noise_ref,
    order_ref,
    near_ref,
    within_ref,
    across_ref,
    coup_ref,
    gain_ref,
    resid_ref,
    cbuf,
    fld0,
    fld1,
    packed,
    tiles,
    ft,
    g_own,
    basis,
    acc,
    r1_ref,
    spread_ref,
    c_send,
    c_recv,
    f_send,
    f_recv,
    z_send,
    z_recv,
    p_send,
    p_recv,
):
    leaves = n_group * n_leaf
    cols, pts = obs_ref.shape
    blocks = pts // BLOCK
    group = lax.axis_index("group")
    leaf = lax.axis_index("leaf")
    me = group * n_leaf + leaf
    odd = lax.rem(me, 2)
    delta = 1 - 2 * odd

    def place(index):
        return (index // n_leaf, lax.rem(index, n_leaf))

    def at_offset(k):
        return place(lax.rem(me + k + leaves, leaves))

    partner = place(me + delta)

    barrier = pltpu.get_barrier_semaphore()
    peers = [at_offset(k) for k in HOPS] + [partner]
    peers += [(group, lax.rem(leaf + 2 * t, n_leaf)) for t in range(1, n_leaf // 2)]
    peers += [(lax.rem(group + t, n_group), leaf) for t in range(1, n_group)]
    for peer in peers:
        pl.semaphore_signal(barrier, inc=1, device_id=peer, device_id_type=MESH)

    def exchange(buf, send, recv):
        def copy(source, target, which, device):
            return pltpu.make_async_remote_copy(
                src_ref=buf.at[source],
                dst_ref=buf.at[target],
                send_sem=send.at[which],
                recv_sem=recv.at[which],
                device_id=device,
                device_id_type=MESH,
            )

        far = [copy(REACH, REACH - k, n, at_offset(k)) for n, k in enumerate(HOPS)]
        own = copy(REACH, REACH - delta, 4, partner)
        moved = (-2, 2, 4 * delta)
        on = [copy(REACH + e, REACH + e - delta, 5 + n, partner) for n, e in enumerate(moved)]
        back = (-2, 2, -4 * delta)
        arriving = [copy(REACH, REACH + delta, 4, partner)] + [
            copy(REACH, REACH + e + delta, 5 + n, partner) for n, e in enumerate(back)
        ]

        def start():
            for c in (far[1], far[2], own, far[0], far[3]):
                c.start()

        def forward():
            far[2].wait_recv()
            on[0].start()
            far[1].wait_recv()
            on[1].start()
            far[0].wait_recv()
            far[3].wait_recv()
            on[2].start()

        def finish():
            for c in arriving:
                c.wait_recv()

        def drain():
            for c in far + [own] + on:
                c.wait_send()

        return start, forward, finish, drain

    coord_x = exchange(cbuf, c_send, c_recv)
    field0 = exchange(fld0, f_send.at[0], f_recv.at[0])
    field1 = [
        exchange(fld1[b], f_send.at[1 + b], f_recv.at[1 + b]) for b in range(blocks)
    ]

    def far_exchange(it):
        first = [
            pltpu.make_async_remote_copy(
                src_ref=packed[it].at[leaf, group],
                dst_ref=packed[it].at[leaf, group],
                send_sem=z_send.at[it, t],
                recv_sem=z_recv.at[it, t],
                device_id=(lax.rem(group + t, n_group), leaf),
                device_id_type=MESH,
            )
            for t in range(1, n_group)
        ]
        def slab(source, which, device):
            return pltpu.make_async_remote_copy(
                src_ref=packed[it].at[source],
                dst_ref=packed[it].at[source],
                send_sem=p_send.at[it, which],
                recv_sem=p_recv.at[it, which],
                device_id=device,
                device_id_type=MESH,
            )

        mate = leaf + delta
        others = [lax.rem(leaf + 2 * t, n_leaf) for t in range(1, n_leaf // 2)]
        back = [lax.rem(leaf - 2 * t + n_leaf, n_leaf) for t in range(1, n_leaf // 2)]
        second = [slab(leaf, 2 * t, (group, o)) for t, o in enumerate(others)]
        arriving = [slab(o, 2 * t, (group, o)) for t, o in enumerate(back)]
        own = slab(leaf, n_leaf - 1, (group, mate))
        third = [slab(o, 2 * t + 1, (group, mate)) for t, o in enumerate(back)]
        last = [slab(o + delta, 2 * t + 1, (group, mate)) for t, o in enumerate(back)]
        last.append(slab(mate, n_leaf - 1, (group, mate)))

        def start():
            for c in first:
                c.start()

        def forward():
            for c in first:
                c.wait_recv()
            for c in second + [own]:
                c.start()

        def pass_on():
            for a, c in zip(arriving, third):
                a.wait_recv()
                c.start()

        def finish():
            for c in last:
                c.wait_recv()

        def drain():
            for c in first + second + third + [own]:
                c.wait_send()

        return start, forward, pass_on, finish, drain

    far0, far1 = far_exchange(0), far_exchange(1)

    slot_row = lax.broadcasted_iota(jnp.int32, (pts, pts), 0)
    pick = jnp.where(slot_row == order_ref[...], 1.0, 0.0).astype(BF16)
    raw = eight(coords_ref[...])
    pieces = jnp.concatenate(list(split3(raw)), axis=0).astype(BF16)
    moved = dot_last(pieces, pick)
    mine = (moved[:ROWS] + moved[ROWS : 2 * ROWS]) + moved[2 * ROWS :]
    cbuf[REACH] = mine[:3]

    centre = (upper_bound + lower_bound) / 2.0
    half_width = (upper_bound - lower_bound) / 2.0
    ratio0 = 1.0 / (centre / half_width)
    ratio1 = 1.0 / (2.0 * centre / half_width - ratio0)

    def block_of(b):
        return slice(b * BLOCK, (b + 1) * BLOCK)

    for b in range(blocks):
        fld0[REACH, b] = (obs_ref[:, block_of(b)] / centre).astype(BF16)
    pl.semaphore_wait(barrier, len(peers))
    coord_x[0]()
    field0[0]()

    shift0 = (me.astype(F32) + 0.5) * SLAB
    source, target = features(mine, shift0)
    g_own[...] = target.astype(BF16)
    ft[0] = source.T.astype(BF16)
    rank = prox_ref.shape[2]
    prox = eight(jnp.concatenate([prox_ref[r] for r in range(3)], axis=0))
    prox = jnp.concatenate([prox, jnp.zeros((ROWS, 128 - rank), F32)], axis=1)
    prox_source, _ = features(prox, shift0)
    prox_t = prox_source.T.astype(BF16)[:rank]
    basis[...] = from_squares(dot(prox_t, g_own[...]))

    def field(it, slot, b):
        return fld0[slot, b] if it == 0 else fld1[b][slot]

    def pack(it):
        total = None
        for b in range(blocks):
            part = dot_last(field(it, REACH, b), basis[:, block_of(b)])
            total = part if total is None else total + part
        half = cols // 2
        packed[it][leaf, group] = jnp.concatenate(
            [total[:half], total[half:]], axis=1
        ).astype(BF16)

    pack(0)
    far0[0]()

    def build(j, b, diagonal, slot=None):
        right = g_own[:, block_of(b)]
        total = None
        for c in range(pts // BLOCK):
            rows = slice(c * BLOCK, (c + 1) * BLOCK)
            s = dot(ft[j, rows, :], right)
            if diagonal and c == b:
                at = lax.broadcasted_iota(jnp.int32, s.shape, 0)
                to = lax.broadcasted_iota(jnp.int32, s.shape, 1)
                s = jnp.where(at == to, 0.0, s)
            tile = from_squares(s)
            tiles[j, b, rows, :] = tile
            if slot is not None:
                part = dot(field(0, slot, c), tile)
                total = part if total is None else total + part
        return total

    for b in range(blocks):
        build(0, b, True)

    coord_x[1]()
    coord_x[2]()
    near_count = near_ref.shape[1]

    def slot_of(j):
        return jnp.minimum(lax.rem(near_ref[0, j] - me + REACH + leaves, leaves), SPAN - 1)

    def stack(j, carry):
        source, _ = features(eight(cbuf[slot_of(j)]), shift0)
        ft[j + 1] = source.T.astype(BF16)
        return carry

    lax.fori_loop(0, near_count, stack, 0)

    def build_near(b):
        def one(j, carry):
            build(j + 1, b, False)
            return carry

        for j in range(near_count):
            one(j, 0)

    def build_apply(b):
        total = term(0, b, range(blocks), REACH, 0)
        for j in range(near_count):
            total = total + build(j + 1, b, False, slot_of(j))
        return total

    def term(it, b, ks, slot, j):
        total = None
        for k in ks:
            part = dot(field(it, slot, k), tiles[j, b, k * BLOCK : (k + 1) * BLOCK, :])
            total = part if total is None else total + part
        return total

    def near(it, b, ks):
        def one(j, total):
            return total + term(it, b, ks, slot_of(j), j + 1)

        total = term(it, b, ks, REACH, 0)
        for j in range(near_count):
            total = one(j, total)
        return total

    def spread(it):
        total = None
        n_within = within_ref.shape[1]
        n_across = across_ref.shape[0]
        for f in range(coup_ref.shape[0]):
            if f < n_within:
                block = packed[it][within_ref[0, f], group]
            else:
                k, a = divmod(f - n_within, n_across)
                block = packed[it][across_ref[a, k], lax.rem(group + 1 + k, n_group)]
            block = jnp.concatenate([block[:, :rank], block[:, rank:]], axis=0)
            part = dot_last(block, coup_ref[f])
            total = part if total is None else total + part
        spread_ref[...] = total.astype(BF16)

    def step0(b, total):
        cut = block_of(b)
        near_part = total + dot(spread_ref[...], basis[:, cut])
        obs = obs_ref[:, cut]
        d0 = obs / centre
        res = obs - (noise_ref[:, cut] * d0 + near_part / kernel_scale)
        d1 = ratio1 * ratio0 * d0 + 2.0 * ratio1 / half_width * res
        fld1[b][REACH] = d1.astype(BF16)
        field1[b][0]()
        r1_ref[:, cut] = res - noise_ref[:, cut] * d1
        gain_ref[:, cut] = d0 + d1

    head = max(1, blocks // 2)
    for b in range(head):
        build_near(b)
        if b == 0:
            field0[1]()
            far0[1]()
            if head == 1:
                far0[2]()
        else:
            far0[2]()
    field0[2]()
    far0[3]()
    spread(0)
    for b in range(head):
        step0(b, near(0, b, range(blocks)))
    for b in range(head, blocks):
        step0(b, build_apply(b))
        for e in range(0 if b == head else b - 1, b):
            field1[e][1]()
    pack(1)
    far1[0]()
    for e in range(blocks - 1):
        field1[e][2]()
    for b in range(blocks):
        acc[:, block_of(b)] = near(1, b, range(blocks - 1))
        if b == 0:
            field1[blocks - 1][1]()
        if b == blocks // 2 - 1:
            far1[1]()
    far1[2]()
    field1[blocks - 1][2]()
    for b in range(blocks):
        cut = block_of(b)
        acc[:, cut] = acc[:, cut] + near(1, b, (blocks - 1,))
    far1[3]()
    spread(1)
    for b in range(blocks):
        cut = block_of(b)
        total = acc[:, cut] + dot(spread_ref[...], basis[:, cut])
        resid_ref[:, cut] = r1_ref[:, cut] - total / kernel_scale

    coord_x[3]()
    field0[3]()
    for b in range(blocks):
        field1[b][3]()
    far0[4]()
    far1[4]()


def local(
    n_group,
    n_leaf,
    observations,
    coordinates,
    proxies,
    noise_variance,
    ordering,
    near_list,
    far_within,
    far_across,
    couplings,
):
    cols, pts = observations.shape
    rank = proxies.shape[2]
    blocks = pts // BLOCK
    vmem = pl.BlockSpec(memory_space=pltpu.VMEM)
    smem = pl.BlockSpec(memory_space=pltpu.SMEM)
    dma = pltpu.SemaphoreType.DMA
    return pl.pallas_call(
        functools.partial(kernel, n_group, n_leaf),
        out_shape=(
            jax.ShapeDtypeStruct((cols, pts), F32),
            jax.ShapeDtypeStruct((cols, pts), F32),
        ),
        in_specs=[vmem] * 5 + [smem] * 3 + [vmem],
        out_specs=(vmem, vmem),
        scratch_shapes=[
            pltpu.VMEM((SPAN, 3, pts), F32),
            pltpu.VMEM((SPAN, blocks, cols, BLOCK), BF16),
            [pltpu.VMEM((SPAN, cols, BLOCK), BF16)] * blocks,
            [pltpu.VMEM((n_leaf, n_group, cols // 2, 2 * rank), BF16)] * 2,
            pltpu.VMEM((near_list.shape[1] + 1, blocks, pts, BLOCK), BF16),
            pltpu.VMEM((near_list.shape[1] + 1, pts, DEPTH), BF16),
            pltpu.VMEM((DEPTH, pts), BF16),
            pltpu.VMEM((rank, pts), BF16),
            pltpu.VMEM((cols, pts), F32),
            pltpu.VMEM((cols, pts), F32),
            pltpu.VMEM((cols, rank), BF16),
            dma((8,)),
            dma((8,)),
            dma((1 + blocks, 8)),
            dma((1 + blocks, 8)),
            dma((2, n_group)),
            dma((2, n_group)),
            dma((2, n_leaf)),
            dma((2, n_leaf)),
        ],
        compiler_params=pltpu.CompilerParams(
            collective_id=0, has_side_effects=True, vmem_limit_bytes=56 << 20
        ),
    )(
        observations,
        coordinates,
        jnp.transpose(proxies, (1, 0, 2)),
        noise_variance[None, :],
        ordering,
        near_list,
        far_within,
        jnp.transpose(far_across[0]),
        couplings[0],
    )


def solution(mesh):
    placed = (
        P(None, ("group", "leaf")),
        P(None, ("group", "leaf")),
        P(("group", "leaf"), None, None),
        P(("group", "leaf")),
        P(("group", "leaf"), None),
        P(("group", "leaf"), None),
        P(("group", "leaf"), None),
        P(("group", "leaf"), None, None),
        P(("group", "leaf"), None, None, None),
    )
    return jax.shard_map(
        functools.partial(local, mesh.shape["group"], mesh.shape["leaf"]),
        mesh=mesh,
        in_specs=placed,
        out_specs=(P(None, ("group", "leaf")), P(None, ("group", "leaf"))),
        check_vma=False,
    )
```

profile of v0, /device:TPU:1, one launch (start us, length us, event | category | flops | bytes accessed | tf_op | source)
XLA Modules:
  0.0 49.3 jit_solution(336523669987619269)
XLA Ops:
  0.6 46.2 %shard_map.104 = (f32[64,1024]{1,0:T(8,128)}, f32[64,1024]{1,0:T(8,128)}) custom-call(f32[64,1024]{1,0:T(8,128)} %obs_ref.1, f32[3,1024]{1,0:T(4,128)} %coords_ref.1, f32[3,1,64]{2,1,0:T(1,128)} %bitcast.8, f32[1,1024]{1,0:T(1,128)} %bitcast.7, s32[1,1024]{1,0:T(1,128)} %order_ref.1, s32[1,7]{1,0:T(1,128)} %near_ref.1, s32[1,6]{1,0:T(1,128)} %within_ref.1, ...), custom_call_target="tpu_custom_call" | custom-call | tf_op jit(solution)/shard_map/pallas_call | solution.py:452
  46.9 0.0 copy-start
  46.9 1.7 %copy.13 = f32[64,1024]{1,0:T(8,128)} copy(f32[64,1024]{1,0:T(8,128)} %get-tuple-element.4) | data formatting | bytes 524288
  48.6 0.0 copy-done
  48.6 0.7 %copy.14 = f32[64,1024]{1,0:T(8,128)} copy(f32[64,1024]{1,0:T(8,128)S(1)} %copy-done) | data formatting | bytes 524288
Async XLA Ops:
  46.9 1.7 %copy-start = (f32[64,1024]{1,0:T(8,128)S(1)}, f32[64,1024]{1,0:T(8,128)}, u32[]{:S(2)}) copy-start(f32[64,1024]{1,0:T(8,128)} %get-tuple-element.5) | copy-start | bytes 786436
where the time goes:
time: 49.5 us; the launch traced here: 49.3 us
  Pallas kernels  46.2 us (93%)
  local copies, waits for them, and re-layouts  2.42 us (5%)
  between operations  0.65 us (1%)
    pallas_call x1, Pallas kernels, local(): pl.pallas_call(functools.partial(kernel, n_group, n_leaf), out_shape=(jax...  46.2 us
    unnamed x4, local copies, waits for them, and re-layouts  2.42 us

commit v1 on v0

v1 whole, which is shorter than its diff:
```python
import functools
import math

import jax
import jax.numpy as jnp
from jax import lax
from jax.experimental import pallas as pl
from jax.experimental.pallas import tpu as pltpu
from jax.sharding import PartitionSpec as P

length_scale = 0.5
kernel_scale = 8.0
lower_bound = 0.5
upper_bound = 4.0
REACH = 4
SPAN = 2 * REACH + 1
SLAB = 0.25
SIDE = 8.0
SCALE = 1.0 / (length_scale * math.log(2.0))
TINY = 1e-12
BLOCK = 256
ROWS = 8
DEPTH = 128
RELAYED = ()
VMEM_LIMIT = 56 << 20
MESH = pl.DeviceIdType.MESH
F32 = jnp.float32
BF16 = jnp.bfloat16

LAST = (((1,), (1,)), ((), ()))


def dot(a, b):
    return jnp.dot(a, b, preferred_element_type=F32)


def dot_last(a, b):
    return lax.dot_general(a, b, LAST, preferred_element_type=F32)


def split3(x):
    high = x.astype(BF16).astype(F32)
    rest = x - high
    mid = rest.astype(BF16).astype(F32)
    low = (rest - mid).astype(BF16).astype(F32)
    return high, mid, low


def eight(coords):
    return jnp.concatenate(
        [coords, jnp.zeros((ROWS - coords.shape[0], coords.shape[1]), F32)], axis=0
    )


def features(coords, shift0):
    row = lax.broadcasted_iota(jnp.int32, coords.shape, 0)
    shift = jnp.where(row == 0, shift0, SIDE / 2)
    x = jnp.where(row < 3, (coords - shift) * SCALE, 0.0)
    h, m, l = split3(x)
    n1, n2, n3 = split3(jnp.sum(x * x, axis=0, keepdims=True))
    one = jnp.ones_like(x)
    zero = jnp.zeros_like(x)
    left = jnp.where(row == 0, n1, jnp.where(row == 1, n2, n3))
    left = jnp.where(row < 3, left, jnp.where(row < 6, one, zero))
    right = jnp.where(row == 3, n1, jnp.where(row == 4, n2, n3))
    right = jnp.where(row < 3, one, jnp.where(row < 6, right, zero))
    pad = [zero] * (DEPTH // ROWS - 10)
    source = jnp.concatenate([h, h, h, m, m, m, l, l, l, left] + pad, axis=0)
    h2, m2, l2 = -2.0 * h, -2.0 * m, -2.0 * l
    target = jnp.concatenate([h2, m2, l2, h2, m2, l2, h2, m2, l2, right] + pad, axis=0)
    return source, target


def from_squares(s):
    s = jnp.maximum(s, TINY)
    return jnp.exp2(-(s * lax.rsqrt(s))).astype(BF16)


def kernel(
    n_group,
    n_leaf,
    obs_hbm,
    coords_hbm,
    prox_hbm,
    noise_hbm,
    order_hbm,
    near_hbm,
    within_hbm,
    across_hbm,
    coup_hbm,
    gain_ref,
    resid_ref,
    obs_ref,
    coords_ref,
    prox_ref,
    noise_ref,
    order_ref,
    near_ref,
    within_ref,
    across_ref,
    coup_ref,
    cbuf,
    fld0,
    fld1,
    packed,
    tiles,
    ft,
    g_own,
    basis,
    acc,
    r1_ref,
    spread_ref,
    in_sem,
    c_send,
    c_recv,
    f_send,
    f_recv,
    z_send,
    z_recv,
    p_send,
    p_recv,
):
    leaves = n_group * n_leaf
    chips = leaves // 2
    cols, pts = obs_ref.shape
    blocks = pts // BLOCK
    halves = 2
    group = lax.axis_index("group")
    leaf = lax.axis_index("leaf")
    me = group * n_leaf + leaf
    odd = lax.rem(me, 2)
    delta = 1 - 2 * odd
    place_in_four = lax.rem(me // 2, 4)
    ex = 2 * (1 - 2 * lax.rem(place_in_four, 2))
    ey = 4 * (1 - 2 * (place_in_four // 2))

    def place(index):
        return (index // n_leaf, lax.rem(index, n_leaf))

    def at_offset(k):
        return place(lax.rem(me + k + leaves, leaves))

    partner = place(me + delta)

    barrier = pltpu.get_barrier_semaphore()
    near_offsets = [k for k in range(-REACH, REACH + 1) if k != 0]
    peers = [at_offset(k) for k in near_offsets if k % 2]
    peers += [at_offset(2 * t) for t in range(1, chips)]
    for peer in peers:
        pl.semaphore_signal(barrier, inc=1, device_id=peer, device_id_type=MESH)

    loads = [
        pltpu.make_async_copy(source, target, in_sem.at[n])
        for n, (source, target) in enumerate(
            (
                (order_hbm, order_ref),
                (coords_hbm, coords_ref),
                (obs_hbm, obs_ref),
                (prox_hbm, prox_ref),
                (near_hbm, near_ref),
                (within_hbm, within_ref),
                (across_hbm, across_ref),
                (noise_hbm, noise_ref),
                (coup_hbm, coup_ref),
            )
        )
    ]
    for c in loads:
        c.start()

    def remote(source, target, send, recv, device):
        return pltpu.make_async_remote_copy(
            src_ref=source,
            dst_ref=target,
            send_sem=send,
            recv_sem=recv,
            device_id=device,
            device_id_type=MESH,
        )

    def coord_copy(n, source, target, device):
        return remote(cbuf.at[source], cbuf.at[target], c_send.at[n], c_recv.at[n], device)

    coord_out = [
        coord_copy(n, REACH, REACH - k, at_offset(k)) for n, k in enumerate(near_offsets)
    ]
    coord_order = sorted(range(len(near_offsets)), key=lambda n: -abs(near_offsets[n]))

    class Exchange:
        def __init__(self, view, send, recv, relayed):
            def copy(source, target, which, device):
                return remote(
                    view(source), view(target), send.at[which], recv.at[which], device
                )

            self.relayed = relayed
            self.y = copy(REACH, REACH - ey, 1, at_offset(ey))
            self.x = copy(REACH, REACH - ex, 0, at_offset(ex))
            self.b = copy(REACH, REACH + ex, 2, at_offset(-ex))
            if relayed:
                self.a = copy(REACH + ey, REACH - ey, 3, at_offset(2 * ey))
            else:
                self.a = copy(REACH, REACH + ey, 3, at_offset(-ey))
            self.own = copy(REACH, REACH - delta, 4, partner)
            moved = (ex, -ex, 4 * delta)
            self.on = [
                copy(REACH + e, REACH + e - delta, 5 + n, partner)
                for n, e in enumerate(moved)
            ]
            back = (ex, -ex, -4 * delta)
            self.arriving = [copy(REACH, REACH + delta, 4, partner)] + [
                copy(REACH, REACH + e + delta, 5 + n, partner) for n, e in enumerate(back)
            ]

        def start(self):
            self.y.start()
            if not self.relayed:
                self.a.start()

        def start_rest(self):
            self.x.start()
            self.b.start()
            self.own.start()

        def relay(self):
            self.y.wait_recv()
            if self.relayed:
                self.a.start()

        def forward_x(self):
            self.x.wait_recv()
            self.on[0].start()

        def forward_b(self):
            self.b.wait_recv()
            self.on[1].start()

        def forward_a(self):
            self.a.wait_recv()
            self.on[2].start()

        def finish(self):
            for c in self.arriving:
                c.wait_recv()

        def drain(self):
            for c in [self.y, self.x, self.b, self.a, self.own] + self.on:
                c.wait_send()

    span = blocks // halves

    def half_view(h):
        return lambda slot: fld0.at[slot, pl.ds(h * span, span)]

    def block_view(b):
        return lambda slot: fld1[b].at[slot]

    field0 = [
        Exchange(half_view(h), f_send.at[h], f_recv.at[h], True) for h in range(halves)
    ]
    field1 = [
        Exchange(block_view(b), f_send.at[halves + b], f_recv.at[halves + b], b in RELAYED)
        for b in range(blocks)
    ]

    class Far:
        def __init__(self, it):
            def block(index):
                return packed[it].at[lax.rem(index, n_leaf), index // n_leaf]

            def shifted(t):
                return lax.rem(me + 2 * t, leaves)

            self.out = [
                remote(block(me), block(me), z_send.at[it, t], z_recv.at[it, t], place(shifted(t)))
                for t in range(1, chips)
            ]
            def slab(source, which):
                return remote(
                    packed[it].at[source],
                    packed[it].at[source],
                    p_send.at[it, which],
                    p_recv.at[it, which],
                    partner,
                )

            own = [lax.rem(leaf + 2 * t, n_leaf) for t in range(n_leaf // 2)]
            self.on = [slab(o, t) for t, o in enumerate(own)]
            self.last = [slab(o + delta, t) for t, o in enumerate(own)]

        def start(self):
            for c in self.out:
                c.start()

        def forward(self):
            for c in self.out:
                c.wait_recv()
            for c in self.on:
                c.start()

        def finish(self):
            for c in self.last:
                c.wait_recv()

        def drain(self):
            for c in self.out + self.on:
                c.wait_send()

    far0, far1 = Far(0), Far(1)

    loads[0].wait()
    loads[1].wait()
    slot_row = lax.broadcasted_iota(jnp.int32, (pts, pts), 0)
    pick = jnp.where(slot_row == order_ref[...], 1.0, 0.0).astype(BF16)
    raw = eight(coords_ref[...])
    pieces = jnp.concatenate(list(split3(raw)), axis=0).astype(BF16)
    moved = dot_last(pieces, pick)
    mine = (moved[:ROWS] + moved[ROWS : 2 * ROWS]) + moved[2 * ROWS :]
    cbuf[REACH] = mine[:3]

    centre = (upper_bound + lower_bound) / 2.0
    half_width = (upper_bound - lower_bound) / 2.0
    ratio0 = 1.0 / (centre / half_width)
    ratio1 = 1.0 / (2.0 * centre / half_width - ratio0)

    def block_of(b):
        return slice(b * BLOCK, (b + 1) * BLOCK)

    loads[2].wait()
    for b in range(blocks):
        fld0[REACH, b] = (obs_ref[:, block_of(b)] / centre).astype(BF16)
    pl.semaphore_wait(barrier, len(peers))
    for n in coord_order:
        coord_out[n].start()
    for h in range(halves):
        field0[h].start()

    shift0 = (me.astype(F32) + 0.5) * SLAB
    source, target = features(mine, shift0)
    g_own[...] = target.astype(BF16)
    ft[0] = source.T.astype(BF16)
    for c in loads[3:]:
        c.wait()
    rank = prox_ref.shape[2]
    prox = eight(jnp.concatenate([prox_ref[r] for r in range(3)], axis=0))
    prox = jnp.concatenate([prox, jnp.zeros((ROWS, 128 - rank), F32)], axis=1)
    prox_source, _ = features(prox, shift0)
    prox_t = prox_source.T.astype(BF16)[:rank]
    basis[...] = from_squares(dot(prox_t, g_own[...]))

    def field(it, slot, b):
        return fld0[slot, b] if it == 0 else fld1[b][slot]

    def pack(it):
        total = None
        for b in range(blocks):
            part = dot_last(field(it, REACH, b), basis[:, block_of(b)])
            total = part if total is None else total + part
        half = cols // 2
        packed[it][leaf, group] = jnp.concatenate(
            [total[:half], total[half:]], axis=1
        ).astype(BF16)

    pack(0)
    far0.start()
    for h in range(halves):
        field0[h].start_rest()

    def build(j, b, diagonal, slot=None):
        right = g_own[:, block_of(b)]
        total = None
        for c in range(pts // BLOCK):
            rows = slice(c * BLOCK, (c + 1) * BLOCK)
            s = dot(ft[j, rows, :], right)
            if diagonal and c == b:
                at = lax.broadcasted_iota(jnp.int32, s.shape, 0)
                to = lax.broadcasted_iota(jnp.int32, s.shape, 1)
                s = jnp.where(at == to, 0.0, s)
            tile = from_squares(s)
            tiles[j, b, rows, :] = tile
            if slot is not None:
                part = dot(field(0, slot, c), tile)
                total = part if total is None else total + part
        return total

    for b in range(blocks):
        build(0, b, True)

    for n in coord_order:
        coord_out[n].wait_recv()
    near_count = near_ref.shape[1]

    def slot_of(j):
        return jnp.minimum(lax.rem(near_ref[0, j] - me + REACH + leaves, leaves), SPAN - 1)

    def stack(j, carry):
        source, _ = features(eight(cbuf[slot_of(j)]), shift0)
        ft[j + 1] = source.T.astype(BF16)
        return carry

    lax.fori_loop(0, near_count, stack, 0)

    def build_near(b, after):
        for j in range(near_count):
            build(j + 1, b, False)
            for act in after.get(j, ()):
                act()

    def build_apply(b, after):
        total = term(0, b, range(blocks), REACH, 0)
        for j in range(near_count):
            total = total + build(j + 1, b, False, slot_of(j))
            for act in after.get(j, ()):
                act()
        return total

    def term(it, b, ks, slot, j):
        total = None
        for k in ks:
            part = dot(field(it, slot, k), tiles[j, b, k * BLOCK : (k + 1) * BLOCK, :])
            total = part if total is None else total + part
        return total

    def near(it, b, ks):
        total = term(it, b, ks, REACH, 0)
        for j in range(near_count):
            total = total + term(it, b, ks, slot_of(j), j + 1)
        return total

    def spread(it):
        total = None
        n_within = within_ref.shape[1]
        n_across = across_ref.shape[0]
        for f in range(coup_ref.shape[0]):
            if f < n_within:
                block = packed[it][within_ref[0, f], group]
            else:
                k, a = divmod(f - n_within, n_across)
                block = packed[it][across_ref[a, k], lax.rem(group + 1 + k, n_group)]
            block = jnp.concatenate([block[:, :rank], block[:, rank:]], axis=0)
            part = dot_last(block, coup_ref[f])
            total = part if total is None else total + part
        spread_ref[...] = total.astype(BF16)

    def step0(b, total):
        cut = block_of(b)
        near_part = total + dot(spread_ref[...], basis[:, cut])
        obs = obs_ref[:, cut]
        d0 = obs / centre
        res = obs - (noise_ref[:, cut] * d0 + near_part / kernel_scale)
        d1 = ratio1 * ratio0 * d0 + 2.0 * ratio1 / half_width * res
        fld1[b][REACH] = d1.astype(BF16)
        if b < blocks - 1:
            field1[b].start()
            field1[b].start_rest()
        r1_ref[:, cut] = res - noise_ref[:, cut] * d1
        gain_ref[:, cut] = d0 + d1

    def near_early(b, count):
        total = term(0, b, range(blocks), REACH, 0)
        for j in range(count):
            total = total + term(0, b, range(blocks), slot_of(j), j + 1)
        return total

    f0, f1 = field0
    build_near(0, {4: (f0.relay,)})
    f1.relay()
    build_near(1, {1: (f0.forward_x, f1.forward_x)})
    build_near(2, {1: (far0.forward,), 4: (f0.forward_b, f1.forward_b)})
    last = blocks - 1
    early = 3
    for j in range(early):
        build(j + 1, last, False)
        if j == 0:
            f0.forward_a()
            f1.forward_a()
    far0.finish()
    spread(0)
    f0.finish()
    f1.finish()
    for b in range(blocks - 1):
        step0(b, near(0, b, range(blocks)))
    total = near_early(last, early)
    acts = {3: (field1[0].relay,), 5: (field1[1].relay,)}
    for j in range(early, near_count):
        total = total + build(j + 1, last, False, slot_of(j))
        for act in acts.get(j, ()):
            act()
    for j in acts:
        if j < early:
            for act in acts[j]:
                act()
    step0(last, total)
    field1[3].start()
    field1[3].start_rest()
    pack(1)
    far1.start()
    field1[2].relay()
    for b in range(blocks):
        acc[:, block_of(b)] = term(1, b, range(blocks), REACH, 0)
    for e in field1[:2]:
        e.forward_x()
        e.forward_b()
    field1[0].forward_a()

    def late(ks):
        for b in range(blocks):
            cut = block_of(b)
            total = acc[:, cut]
            for j in range(near_count):
                total = total + term(1, b, ks, slot_of(j), j + 1)
            acc[:, cut] = total

    field1[1].forward_a()
    field1[0].finish()
    late((0,))
    field1[2].forward_x()
    field1[2].forward_b()
    field1[2].forward_a()
    field1[1].finish()
    late((1,))
    field1[3].relay()
    field1[3].forward_x()
    field1[3].forward_b()
    field1[3].forward_a()
    field1[2].finish()
    late((2,))
    far1.forward()
    field1[3].finish()
    late((3,))
    far1.finish()
    spread(1)

    for b in range(blocks):
        cut = block_of(b)
        total = acc[:, cut] + dot(spread_ref[...], basis[:, cut])
        resid_ref[:, cut] = r1_ref[:, cut] - total / kernel_scale

    for c in coord_out:
        c.wait_send()
    for e in field0 + field1:
        e.drain()
    far0.drain()
    far1.drain()


def local(
    n_group,
    n_leaf,
    observations,
    coordinates,
    proxies,
    noise_variance,
    ordering,
    near_list,
    far_within,
    far_across,
    couplings,
):
    operands = (
        observations,
        coordinates,
        jnp.transpose(proxies, (1, 0, 2)),
        noise_variance[None, :],
        ordering,
        near_list,
        far_within,
        jnp.transpose(far_across[0]),
        couplings[0],
    )
    cols, pts = observations.shape
    rank = proxies.shape[2]
    blocks = pts // BLOCK
    chips = n_group * n_leaf // 2
    vmem = pl.BlockSpec(memory_space=pltpu.VMEM)
    dma = pltpu.SemaphoreType.DMA
    spaces = [pltpu.VMEM] * 5 + [pltpu.SMEM] * 3 + [pltpu.VMEM]
    return pl.pallas_call(
        functools.partial(kernel, n_group, n_leaf),
        out_shape=(
            jax.ShapeDtypeStruct((cols, pts), F32),
            jax.ShapeDtypeStruct((cols, pts), F32),
        ),
        in_specs=[pl.BlockSpec(memory_space=pltpu.HBM)] * len(operands),
        out_specs=(vmem, vmem),
        scratch_shapes=[space(x.shape, x.dtype) for space, x in zip(spaces, operands)]
        + [
            pltpu.VMEM((SPAN, 3, pts), F32),
            pltpu.VMEM((SPAN, blocks, cols, BLOCK), BF16),
            [pltpu.VMEM((SPAN, cols, BLOCK), BF16)] * blocks,
            [pltpu.VMEM((n_leaf, n_group, cols // 2, 2 * rank), BF16)] * 2,
            pltpu.VMEM((near_list.shape[1] + 1, blocks, pts, BLOCK), BF16),
            pltpu.VMEM((near_list.shape[1] + 1, pts, DEPTH), BF16),
            pltpu.VMEM((DEPTH, pts), BF16),
            pltpu.VMEM((rank, pts), BF16),
            pltpu.VMEM((cols, pts), F32),
            pltpu.VMEM((cols, pts), F32),
            pltpu.VMEM((cols, rank), BF16),
            dma((len(operands),)),
            dma((8,)),
            dma((8,)),
            dma((2 + blocks, 8)),
            dma((2 + blocks, 8)),
            dma((2, chips)),
            dma((2, chips)),
            dma((2, n_leaf // 2)),
            dma((2, n_leaf // 2)),
        ],
        compiler_params=pltpu.CompilerParams(
            collective_id=0, has_side_effects=True, vmem_limit_bytes=VMEM_LIMIT
        ),
    )(*operands)


def solution(mesh):
    placed = (
        P(None, ("group", "leaf")),
        P(None, ("group", "leaf")),
        P(("group", "leaf"), None, None),
        P(("group", "leaf")),
        P(("group", "leaf"), None),
        P(("group", "leaf"), None),
        P(("group", "leaf"), None),
        P(("group", "leaf"), None, None),
        P(("group", "leaf"), None, None, None),
    )
    return jax.shard_map(
        functools.partial(local, mesh.shape["group"], mesh.shape["leaf"]),
        mesh=mesh,
        in_specs=placed,
        out_specs=(P(None, ("group", "leaf")), P(None, ("group", "leaf"))),
        check_vma=False,
    )
```

time: 49.5 us -> 45.5 us (0.919)
  Pallas kernels: 46.2 us -> 42.2 us
    pallas_call x1, Pallas kernels: 46.2 us -> 42.2 us  [local(): pl.pallas_call(functools.partial(kernel, n_group, n_leaf), out_shape=(jax...]
where the time goes in v1:
time: 45.5 us; the launch traced here: 45.3 us
  Pallas kernels  42.2 us (93%)
  local copies, waits for them, and re-layouts  2.42 us (5%)
  between operations  0.65 us (1%)
    pallas_call x1, Pallas kernels, local(): pl.pallas_call(functools.partial(kernel, n_group, n_leaf), out_shape=(jax...  42.2 us
    unnamed x4, local copies, waits for them, and re-layouts  2.42 us

profile of v1, /device:TPU:1, one launch (start us, length us, event | category | flops | bytes accessed | tf_op | source)
XLA Modules:
  0.0 45.3 jit_solution(10757523485594894270)
XLA Ops:
  0.6 42.2 %shard_map.104 = (f32[64,1024]{1,0:T(8,128)}, f32[64,1024]{1,0:T(8,128)}) custom-call(f32[64,1024]{1,0:T(8,128)} %obs_hbm.1, f32[3,1024]{1,0:T(4,128)} %coords_hbm.1, f32[3,1,64]{2,1,0:T(1,128)} %bitcast.8, f32[1,1024]{1,0:T(1,128)} %bitcast.7, s32[1,1024]{1,0:T(1,128)} %order_hbm.1, s32[1,7]{1,0:T(1,128)} %near_hbm.1, s32[1,6]{1,0:T(1,128)} %within_hbm.1, ...), custom_call_target="tpu_custom_call" | custom-call | tf_op jit(solution)/shard_map/pallas_call | solution.py:578
  42.8 0.0 copy-start
  42.9 1.7 %copy.13 = f32[64,1024]{1,0:T(8,128)} copy(f32[64,1024]{1,0:T(8,128)} %get-tuple-element.4) | data formatting | bytes 524288
  44.6 0.0 copy-done
  44.6 0.7 %copy.14 = f32[64,1024]{1,0:T(8,128)} copy(f32[64,1024]{1,0:T(8,128)S(1)} %copy-done) | data formatting | bytes 524288
Async XLA Ops:
  42.8 1.7 %copy-start = (f32[64,1024]{1,0:T(8,128)S(1)}, f32[64,1024]{1,0:T(8,128)}, u32[]{:S(2)}) copy-start(f32[64,1024]{1,0:T(8,128)} %get-tuple-element.5) | copy-start | bytes 786436
